TPU v7x, 32 devices: a whole 2x2x4 slice. The times are simulated.
32 devices in a mesh: dp: 4 (over z), mp: 8 (over y, x, core).
Axes of the slice: x: 2, y: 2, z: 4, core: 2. Of those that a mesh axis runs over, the one named last changes fastest.
Arguments:
- gradients: bfloat16 [4, 2, 768, 2048], P('dp', None, None, 'mp'), may hold values from -4 to 4
- weights: bfloat16 [2, 768, 2048], P(None, None, 'mp'), may hold values from -4 to 4
- projection: float32 [2, 768, 256], replicated, may hold values from -0.21875 to 0.21875
- moment_first: float32 [2, 256, 2048], P(None, 'dp', 'mp'), may hold values from -6 to 6
- moment_second: float32 [2, 256, 2048], P(None, 'dp', 'mp'), may hold values from 0.25 to 4
Outputs:
- new_weights: bfloat16 [2, 768, 2048], P(None, None, 'mp')
- new_first: float32 [2, 256, 2048], P(None, 'dp', 'mp')
- new_second: float32 [2, 256, 2048], P(None, 'dp', 'mp')
- new_bases: float32 [2, 768, 256], replicated
All inputs are finite; a program needn't handle non-finite values.
Results may differ from a plain program's by a relative error of at most 0.0004.
Values may be sent and summed in bfloat16 or wider, within the bound.
A program may use at most 64 MiB of HBM per device.

v0:
```python
import jax
import jax.numpy as jnp
from jax import lax
from jax.sharding import PartitionSpec as P

NS_ITERS = 4
beta_first = 0.5
beta_second = 0.5
adam_eps = 1e-06
learn_rate = 0.1


def newton_schulz(subspace):
    highest = lax.Precision.HIGHEST
    factor = 1.0 / (jnp.sqrt(jnp.sum(subspace * subspace, axis=(1, 2), keepdims=True)) + 1e-06)
    current = subspace * factor
    for sweep in range(NS_ITERS):
        gram = jnp.einsum("ldr,lds->lrs", current, current, precision=highest)
        current = 1.5 * current - 0.5 * jnp.einsum("ldr,lrs->lds", current, gram, precision=highest)
    return current


def back_project(bases_rows, direction_own):
    highest = lax.Precision.HIGHEST
    return jnp.einsum(
        "ldr,lrf->ldf",
        bases_rows,
        lax.all_gather(direction_own, "dp", axis=1, tiled=True),
        precision=highest,
    )


def shards(gradients, weights, projection, moment_first, moment_second):
    highest = lax.Precision.HIGHEST
    local_grad = gradients[0].astype(jnp.float32)
    totals = lax.psum(local_grad, "dp")
    lowrank = jnp.einsum("ldr,ldf->lrf", projection, totals, precision=highest)
    partial_sub = jnp.einsum("ldf,lrf->ldr", totals, lowrank, precision=highest)
    subspace = lax.psum(partial_sub, "mp")
    rank_rows = moment_first.shape[1]
    rank_start = lax.axis_index("dp") * rank_rows
    low_own = lax.dynamic_slice_in_dim(lowrank, rank_start, rank_rows, 1)
    new_first = beta_first * moment_first + (1.0 - beta_first) * low_own
    new_second = beta_second * moment_second + (1.0 - beta_second) * low_own * low_own
    direction_own = new_first / (jnp.sqrt(new_second) + adam_eps)
    width_rows = weights.shape[1] // lax.axis_size("dp")
    row_start = lax.axis_index("dp") * width_rows
    bases_rows = lax.dynamic_slice_in_dim(projection, row_start, width_rows, 1)
    weight_rows = lax.dynamic_slice_in_dim(weights, row_start, width_rows, 1)
    delta_rows = back_project(bases_rows, direction_own)
    updated = (weight_rows.astype(jnp.float32) - learn_rate * delta_rows).astype(jnp.bfloat16)
    new_weights = lax.all_gather(updated, "dp", axis=1, tiled=True)
    new_bases = newton_schulz(subspace)
    return (new_weights, new_first, new_second, new_bases)


def solution(mesh):
    placed = (
        P("dp", None, None, "mp"),
        P(None, None, "mp"),
        P(),
        P(None, "dp", "mp"),
        P(None, "dp", "mp"),
    )
    return jax.shard_map(
        shards,
        mesh=mesh,
        in_specs=placed,
        out_specs=(P(None, None, "mp"), P(None, "dp", "mp"), P(None, "dp", "mp"), P()),
        check_vma=False,
    )
```

profile of v0, /device:TPU:0, one launch (start us, length us, event | category | flops | bytes accessed | tf_op | source)
XLA Modules:
  0.0 174.0 jit_solution(6145538785186923639)
XLA Ops:
  7.2 0.0 copy-start
  7.2 0.0 all-reduce.3.cloned.1.call-start
  7.2 2.5 %bitcast_convert_fusion = f32[2,768,256]{2,1,0:T(8,128)} fusion(bf16[1,2,768,256]{3,2,1,0:T(8,128)(2,1)} %param.5), kind=kLoop, calls=%fused_computation.12 | loop fusion | flops 393216 | bytes 2359296 | tf_op jit(solution)/shard_map/convert_element_type | solution.py:35
  9.7 0.0 all-reduce.3.cloned.1.call-update
  9.8 0.0 all-reduce.5.cloned.1.call-start
  9.8 72.8 %all-reduce.3.cloned.1.call-done = f32[2,768,256]{2,1,0:T(8,128)} async-done(((f32[2,768,256]{2,1,0:T(8,128)}), f32[2,768,256]{2,1,0:T(8,128)}) %all-reduce.3.cloned.1.call-update) | async-done | bytes 1572880 | tf_op jit(solution)/shard_map/psum | solution.py:36
  82.7 0.0 copy-done
  82.7 0.0 copy-start.2
  82.7 4.2 %fusion.11 = f32[2,256,256]{2,1,0:T(8,128)S(1)} fusion(f32[2,768,256]{2,1,0:T(8,128)S(1)} %copy-done, f32[2,768,256]{2,1,0:T(8,128)} %all-reduce.3.cloned.1.call-done), kind=kOutput, calls=%fused_computation.22 | convolution fusion | flops 1207959552 | bytes 3670016 | tf_op jit(solution)/shard_map/ldr,ldf->lrf/dot_general | solution.py:37
  86.9 0.0 copy-done.2
  86.9 2.6 %convolution_bitcast_fusion = f32[2,768,256]{1,2,0:T(8,128)} fusion(f32[2,256,256]{2,1,0:T(8,128)S(1)} %fusion.11, f32[2,768,256]{2,1,0:T(8,128)S(1)} %copy-done.2), kind=kOutput, calls=%fused_computation.5 | convolution fusion | flops 1207959552 | bytes 3670016 | tf_op jit(solution)/shard_map/ldf,lrf->ldr/dot_general | solution.py:38
  89.5 0.0 copy-start.3
  89.5 0.0 all-reduce.5.cloned.1.call-update
  89.5 0.9 copy-done.3
  90.4 0.1 copy-done.4
  90.5 0.8 add_divide_fusion
  91.2 15.7 %all_gather.6 = f32[2,256,256]{2,1,0:T(8,128)S(1)} all-gather(f32[2,64,256]{2,1,0:T(8,128)S(1)} %get-tuple-element.8), channel_id=1, replica_groups=mesh['dp'=4,'mp'=8] {'dp'}, dimensions={1}, use_global_device_ids=true | all-gather | bytes 655360 | tf_op jit(solution)/shard_map/all_gather | solution.py:28
  106.9 1.5 fusion.4
  108.4 18.3 %all_gather.7 = bf16[2,768,256]{2,1,0:T(8,128)(2,1)} all-gather(bf16[2,192,256]{2,1,0:T(8,128)(2,1)S(1)} %fusion.4), channel_id=1, replica_groups=mesh['dp'=4,'mp'=8] {'dp'}, dimensions={1}, use_global_device_ids=true | all-gather | bytes 983040 | tf_op jit(solution)/shard_map/all_gather | solution.py:52
  126.7 20.9 %all-reduce.5.cloned.1.call-done = f32[2,768,256]{1,2,0:T(8,128)} async-done(((f32[2,768,256]{1,2,0:T(8,128)}), f32[2,768,256]{1,2,0:T(8,128)}) %all-reduce.5.cloned.1.call-update) | async-done | bytes 1572880 | tf_op jit(solution)/shard_map/psum | solution.py:39
  147.6 1.8 %multiply_reduce_fusion = f32[2]{0:T(128)S(1)} fusion(f32[2,768,256]{1,2,0:T(8,128)} %all-reduce.5.cloned.1.call-done), kind=kLoop, calls=%fused_computation.4 | loop fusion | flops 786430 | bytes 1572872 | tf_op jit(solution)/shard_map/reduce_sum | solution.py:15
  149.4 0.0 copy-done.1
  149.5 1.8 %fusion = f32[2,256,256]{2,1,0:T(8,128)S(1)} fusion(f32[2,768,256]{1,2,0:T(8,128)S(1)} %copy-done.1, f32[2]{0:T(128)S(1)} %add_divide_fusion.1), kind=kOutput, calls=%fused_computation.6 | convolution fusion | flops 1208352768 | bytes 2097160 | tf_op jit(solution)/shard_map/ldr,lds->lrs/dot_general | solution.py:18
  151.2 2.0 %multiply_subtract_fusion.3 = f32[2,768,256]{1,2,0:T(8,128)S(1)} fusion(f32[2,256,256]{2,1,0:T(8,128)S(1)} %fusion, f32[2,768,256]{1,2,0:T(8,128)S(1)} %copy-done.1, f32[2]{0:T(128)S(1)} %add_divide_fusion.1), kind=kOutput, calls=%fused_computation.3 | convolution fusion | flops 1209925632 | bytes 3670024 | tf_op jit(solution)/shard_map/ldr,lrs->lds/dot_general | solution.py:19
  153.2 1.6 fusion.12
  154.9 1.8 %multiply_subtract_fusion.2 = f32[2,768,256]{1,2,0:T(8,128)S(1)} fusion(f32[2,768,256]{1,2,0:T(8,128)S(1)} %multiply_subtract_fusion.3, f32[2,256,256]{2,1,0:T(8,128)S(1)} %fusion.12), kind=kOutput, calls=%fused_computation.2 | convolution fusion | flops 1209139200 | bytes 3670016 | tf_op jit(solution)/shard_map/ldr,lrs->lds/dot_general | solution.py:19
  156.6 1.6 fusion.13
  158.3 1.8 %multiply_subtract_fusion.1 = f32[2,768,256]{1,2,0:T(8,128)S(1)} fusion(f32[2,768,256]{1,2,0:T(8,128)S(1)} %multiply_subtract_fusion.2, f32[2,256,256]{2,1,0:T(8,128)S(1)} %fusion.13), kind=kOutput, calls=%fused_computation.1 | convolution fusion | flops 1209139200 | bytes 3670016 | tf_op jit(solution)/shard_map/ldr,lrs->lds/dot_general | solution.py:19
  160.1 1.6 fusion.14
  161.7 1.8 %multiply_subtract_fusion = f32[2,768,256]{1,2,0:T(8,128)S(1)} fusion(f32[2,768,256]{1,2,0:T(8,128)S(1)} %multiply_subtract_fusion.1, f32[2,256,256]{2,1,0:T(8,128)S(1)} %fusion.14), kind=kOutput, calls=%fused_computation | convolution fusion | flops 1209139200 | bytes 3670016 | tf_op jit(solution)/shard_map/ldr,lrs->lds/dot_general | solution.py:19
  163.5 1.6 copy.18
  165.1 2.1 %copy.31 = bf16[2,768,256]{2,1,0:T(8,128)(2,1)} copy(bf16[2,768,256]{2,1,0:T(8,128)(2,1)} %all_gather.7) | data formatting | bytes 1572864
  (3 shorter events, 0.0 us)
Async XLA Ops:
  7.2 75.5 %copy-start = (f32[2,768,256]{2,1,0:T(8,128)S(1)}, f32[2,768,256]{2,1,0:T(8,128)}, u32[]{:S(2)}) copy-start(f32[2,768,256]{2,1,0:T(8,128)} %param.7) | copy-start | bytes 4718596
  7.2 75.5 %all-reduce.3.cloned.1.call-start = ((), (), s32[]{:S(2)}) async-start(), calls=%async_computation | async-start | bytes 3145728 | tf_op jit(solution)/shard_map/psum | solution.py:36
  9.8 137.8 %all-reduce.5.cloned.1.call-start = ((), (), s32[]{:S(2)}) async-start(), calls=%async_computation.1 | async-start | bytes 3145728 | tf_op jit(solution)/shard_map/psum | solution.py:39
  82.7 4.2 %copy-start.2 = (f32[2,768,256]{2,1,0:T(8,128)S(1)}, f32[2,768,256]{2,1,0:T(8,128)}, u32[]{:S(2)}) copy-start(f32[2,768,256]{2,1,0:T(8,128)} %all-reduce.3.cloned.1.call-done) | copy-start | bytes 4718596
  89.5 0.9 copy-start.3
  89.5 1.0 copy-start.4
  147.6 1.9 %copy-start.1 = (f32[2,768,256]{1,2,0:T(8,128)S(1)}, f32[2,768,256]{1,2,0:T(8,128)}, u32[]{:S(2)}) copy-start(f32[2,768,256]{1,2,0:T(8,128)} %all-reduce.5.cloned.1.call-done) | copy-start | bytes 4718596
Sparse Core Ops, SparseCore 0:
  10.9 71.6 all-reduce.2
  89.7 57.8 all-reduce.4
where the time goes:
time: 174 us
  waiting for transfers between devices  93.7 us (54%)
  blocking collectives  34 us (20%)
  matrix products  22.3 us (13%)
  between operations  14.1 us (8%)
  other arithmetic  5.1 us (3%)
  local copies, waits for them, and re-layouts  4.67 us (3%)
    psum x1, waiting for transfers between devices, shards(): totals = lax.psum(local_grad, 'dp')  72.8 us
    psum x1, waiting for transfers between devices, shards(): subspace = lax.psum(partial_sub, 'mp')  20.9 us
    all_gather x1, blocking collectives, shards(): new_weights = lax.all_gather(updated, 'dp', axis=1, tiled=True)  18.3 us
    all_gather x1, blocking collectives, back_project(): lax.all_gather(direction_own, 'dp', axis=1, tiled=True)  15.7 us
    dot_general x4, matrix products, newton_schulz(): jnp.einsum('ldr,lrs->lds', current, gram, precision=highest)  7.29 us
    dot_general x4, matrix products, newton_schulz(): gram = jnp.einsum('ldr,lds->lrs', current, current, precision=highest)  6.66 us
    unnamed x12, local copies, waits for them, and re-layouts  4.67 us
    dot_general x1, matrix products, shards(): lowrank = jnp.einsum('ldr,ldf->lrf', projection, totals, precision=highest)  4.21 us
  transfers between devices with their start and end apart: 2, of which 2 were waited for; matrix products, arithmetic and copies ran while one was open for 1% of the time, Pallas kernels for 0%

commit v1 on v0

--- a/solution.py
+++ b/solution.py
@@ -36,7 +36,8 @@
     totals = lax.psum(local_grad, "dp")
     lowrank = jnp.einsum("ldr,ldf->lrf", projection, totals, precision=highest)
     partial_sub = jnp.einsum("ldf,lrf->ldr", totals, lowrank, precision=highest)
-    subspace = lax.psum(partial_sub, "mp")
+    parts = lax.all_gather(partial_sub, "mp")
+    subspace = jnp.sum(parts, axis=0)
     rank_rows = moment_first.shape[1]
     rank_start = lax.axis_index("dp") * rank_rows
     low_own = lax.dynamic_slice_in_dim(lowrank, rank_start, rank_rows, 1)

time: 174 us -> 199 us (1.14)
  waiting for transfers between devices: 93.7 us -> 106 us
  other arithmetic: 5.1 us -> 11.5 us
  matrix products: 22.3 us -> 26.6 us
    all_gather x0 -> x1, waiting for transfers between devices: none -> 33.2 us  [shards(): parts = lax.all_gather(partial_sub, 'mp')]
    psum x1 -> x0, waiting for transfers between devices: 20.9 us -> none  [shards(): subspace = lax.psum(partial_sub, 'mp')]
    reduce_sum x0 -> x1, other arithmetic: none -> 5.6 us  [shards(): subspace = jnp.sum(parts, axis=0)]
    dot_general x4, matrix products: 6.66 us -> 11.5 us  [newton_schulz(): gram = jnp.einsum('ldr,lds->lrs', current, current, precision=highest)]
    unnamed x12 -> x14, local copies, waits for them, and re-layouts: 4.67 us -> 4.23 us
  transfers between devices with their start and end apart: 2 -> 2, of which waited for: 2 -> 2; matrix products, arithmetic and copies ran while one was open for 1% -> 2% of each run, Pallas kernels for 0% -> 0%
where the time goes in v1:
time: 199 us; the launch traced here: 198 us
  waiting for transfers between devices  106 us (53%)
  blocking collectives  34 us (17%)
  matrix products  26.6 us (13%)
  between operations  14.2 us (7%)
  other arithmetic  11.5 us (6%)
  local copies, waits for them, and re-layouts  5.85 us (3%)
    psum x1, waiting for transfers between devices, shards(): totals = lax.psum(local_grad, 'dp')  72.8 us
    all_gather x1, waiting for transfers between devices, shards(): parts = lax.all_gather(partial_sub, 'mp')  33.2 us
    all_gather x1, blocking collectives, shards(): new_weights = lax.all_gather(updated, 'dp', axis=1, tiled=True)  18.3 us
    all_gather x1, blocking collectives, back_project(): lax.all_gather(direction_own, 'dp', axis=1, tiled=True)  15.7 us
    dot_general x4, matrix products, newton_schulz(): gram = jnp.einsum('ldr,lds->lrs', current, current, precision=highest)  11.5 us
    dot_general x4, matrix products, newton_schulz(): jnp.einsum('ldr,lrs->lds', current, gram, precision=highest)  7.9 us
    reduce_sum x1, other arithmetic, shards(): subspace = jnp.sum(parts, axis=0)  5.6 us
    unnamed x14, local copies, waits for them, and re-layouts  4.23 us
  transfers between devices with their start and end apart: 2, of which 2 were waited for; matrix products, arithmetic and copies ran while one was open for 2% of the time, Pallas kernels for 0%

profile of v1, /device:TPU:0, one launch (start us, length us, event | category | flops | bytes accessed | tf_op | source)
XLA Modules:
  0.0 198.2 jit_solution(3828468764391465688)
XLA Ops:
  7.2 0.0 copy-start
  7.2 0.0 all-reduce.2.cloned.1.call-start
  7.2 2.5 %bitcast_convert_fusion = f32[2,768,256]{2,1,0:T(8,128)} fusion(bf16[1,2,768,256]{3,2,1,0:T(8,128)(2,1)} %param.5), kind=kLoop, calls=%fused_computation.12 | loop fusion | flops 393216 | bytes 2359296 | tf_op jit(solution)/shard_map/convert_element_type | solution.py:35
  9.7 0.0 all-reduce.2.cloned.1.call-update
  9.8 0.0 all-gather.3.cloned.1.call-start
  9.8 72.8 %all-reduce.2.cloned.1.call-done = f32[2,768,256]{2,1,0:T(8,128)} async-done(((f32[2,768,256]{2,1,0:T(8,128)}), f32[2,768,256]{2,1,0:T(8,128)}) %all-reduce.2.cloned.1.call-update) | async-done | bytes 1572880 | tf_op jit(solution)/shard_map/psum | solution.py:36
  82.7 4.2 %fusion.11 = f32[2,256,256]{2,1,0:T(8,128)S(1)} fusion(f32[2,768,256]{2,1,0:T(8,128)S(1)} %copy-done, f32[2,768,256]{2,1,0:T(8,128)} %all-reduce.2.cloned.1.call-done), kind=kOutput, calls=%fused_computation.22 | convolution fusion | flops 1207959552 | bytes 3670016 | tf_op jit(solution)/shard_map/ldr,ldf->lrf/dot_general | solution.py:37
  86.9 0.0 copy-start.3
  86.9 0.8 copy-done.3
  87.7 1.5 convolution_bitcast_fusion
  89.2 1.6 copy.11
  90.8 0.0 all-gather.3.cloned.1.call-update
  90.8 0.9 copy-done.4
  91.7 0.1 copy-done.5
  91.7 1.7 add_divide_fusion
  93.4 15.7 %all_gather.12 = f32[2,256,256]{2,1,0:T(8,128)S(1)} all-gather(f32[2,64,256]{2,1,0:T(8,128)S(1)} %get-tuple-element.4), channel_id=1, replica_groups=mesh['dp'=4,'mp'=8] {'dp'}, dimensions={1}, use_global_device_ids=true | all-gather | bytes 655360 | tf_op jit(solution)/shard_map/all_gather | solution.py:28
  109.1 1.5 fusion.4
  110.6 18.3 %all_gather.13 = bf16[2,768,256]{2,1,0:T(8,128)(2,1)} all-gather(bf16[2,192,256]{2,1,0:T(8,128)(2,1)S(1)} %fusion.4), channel_id=1, replica_groups=mesh['dp'=4,'mp'=8] {'dp'}, dimensions={1}, use_global_device_ids=true | all-gather | bytes 983040 | tf_op jit(solution)/shard_map/all_gather | solution.py:53
  128.9 33.2 %all-gather.3.cloned.1.call-done = f32[16,768,256]{2,1,0:T(8,128)} async-done(((f32[2,768,256]{2,1,0:T(8,128)}), f32[16,768,256]{2,1,0:T(8,128)}) %all-gather.3.cloned.1.call-update) | async-done | bytes 12582928 | tf_op jit(solution)/shard_map/all_gather | solution.py:39
  162.1 5.6 %reduce_sum.18 = f32[2,768,256]{2,1,0:T(8,128)S(1)} reduce(f32[8,2,768,256]{3,2,1,0:T(8,128)} %bitcast.24, f32[]{:T(128)} %constant.8.clone.1), dimensions={0}, to_apply=%region_1.0 | reduce | flops 2752512 | bytes 14155780 | tf_op jit(solution)/shard_map/reduce_sum | solution.py:40
  167.7 1.6 copy.15
  169.3 1.7 multiply_reduce_fusion
  171.1 2.8 %fusion = f32[2,256,256]{2,1,0:T(8,128)S(1)} fusion(f32[2,768,256]{2,1,0:T(8,128)S(1)} %reduce_sum.18, f32[2]{0:T(128)S(1)} %add_divide_fusion.1), kind=kOutput, calls=%fused_computation.6 | convolution fusion | flops 1208352768 | bytes 2097160 | tf_op jit(solution)/shard_map/ldr,lds->lrs/dot_general | solution.py:18
  173.9 1.8 multiply_subtract_fusion.3
  175.7 2.8 %fusion.12 = f32[2,256,256]{2,1,0:T(8,128)S(1)} fusion(f32[2,768,256]{2,1,0:T(8,128)S(1)} %multiply_subtract_fusion.3), kind=kOutput, calls=%fused_computation.23 | convolution fusion | flops 1207959552 | bytes 2097152 | tf_op jit(solution)/shard_map/ldr,lds->lrs/dot_general | solution.py:18
  178.5 1.7 multiply_subtract_fusion.2
  180.2 3.0 %fusion.13 = f32[2,256,256]{2,1,0:T(8,128)S(1)} fusion(f32[2,768,256]{2,1,0:T(8,128)S(1)} %multiply_subtract_fusion.2), kind=kOutput, calls=%fused_computation.24 | convolution fusion | flops 1207959552 | bytes 2097152 | tf_op jit(solution)/shard_map/ldr,lds->lrs/dot_general | solution.py:18
  183.2 1.7 multiply_subtract_fusion.1
  184.9 2.8 %fusion.14 = f32[2,256,256]{2,1,0:T(8,128)S(1)} fusion(f32[2,768,256]{2,1,0:T(8,128)S(1)} %multiply_subtract_fusion.1), kind=kOutput, calls=%fused_computation.25 | convolution fusion | flops 1207959552 | bytes 2097152 | tf_op jit(solution)/shard_map/ldr,lds->lrs/dot_general | solution.py:18
  187.7 0.0 copy-start.2
  187.7 2.8 %multiply_subtract_fusion = f32[2,768,256]{2,1,0:T(8,128)} fusion(f32[2,768,256]{2,1,0:T(8,128)S(1)} %multiply_subtract_fusion.1, f32[2,256,256]{2,1,0:T(8,128)S(1)} %fusion.14), kind=kOutput, calls=%fused_computation | convolution fusion | flops 1209139200 | bytes 3670016 | tf_op jit(solution)/shard_map/ldr,lrs->lds/dot_general | solution.py:19
  190.5 0.9 copy.18
  (7 shorter events, 0.0 us)
Async XLA Ops:
  7.2 75.5 %copy-start = (f32[2,768,256]{2,1,0:T(8,128)S(1)}, f32[2,768,256]{2,1,0:T(8,128)}, u32[]{:S(2)}) copy-start(f32[2,768,256]{2,1,0:T(8,128)} %param.7) | copy-start | bytes 4718596
  7.2 75.5 %all-reduce.2.cloned.1.call-start = ((), (), s32[]{:S(2)}) async-start(), calls=%async_computation | async-start | bytes 3145728 | tf_op jit(solution)/shard_map/psum | solution.py:36
  9.8 152.4 %all-gather.3.cloned.1.call-start = ((), (), s32[]{:S(2)}) async-start(), calls=%async_computation.1 | async-start | bytes 14155776 | tf_op jit(solution)/shard_map/all_gather | solution.py:39
  82.7 5.0 %copy-start.1 = (f32[2,768,256]{2,1,0:T(8,128)S(1)}, f32[2,768,256]{2,1,0:T(8,128)}, u32[]{:S(2)}) copy-start(f32[2,768,256]{2,1,0:T(8,128)} %all-reduce.2.cloned.1.call-done) | copy-start | bytes 4718596
  86.9 0.8 copy-start.3
  90.8 0.9 copy-start.4
  90.8 1.0 copy-start.5
  187.7 2.8 %copy-start.2 = (bf16[2,768,256]{2,1,0:T(8,128)(2,1)S(1)}, bf16[2,768,256]{2,1,0:T(8,128)(2,1)}, u32[]{:S(2)}) copy-start(bf16[2,768,256]{2,1,0:T(8,128)(2,1)} %all_gather.13) | copy-start | bytes 2359300
Sparse Core Ops, SparseCore 0:
  10.9 71.6 all-reduce.1
  90.9 71.1 all-gather.2
